TPU v7x, 256 devices: a whole 4x4x8 slice. The times are simulated.
256 devices in a mesh: layer: 8 (over z_hi, y), row: 32 (over x, z_lo, core).
Axes of the slice: x: 4, y: 4, z: 8 (z_hi: 2, z_lo: 4; z = z_hi * 4 + z_lo), core: 2. Of those that a mesh axis runs over, the one named last changes fastest.
Arguments:
- query_grads: bfloat16 [16, 1024, 4096], P('layer', 'row'), may hold values from -6 to 6
- train_grads: bfloat16 [16, 16384, 4096], P('layer', 'row'), may hold values from -0.023925781 to 0.023925781
- left_inverse: float32 [16, 64, 64], P('layer'), may hold values from -0.75 to 0.75
- right_inverse: float32 [16, 64, 64], P('layer'), may hold values from -0.75 to 0.75
Outputs:
- scores: float32 [1024, 16384], P('layer', 'row')
All inputs are finite; a program needn't handle non-finite values.
Results may differ from a plain program's by a relative error of at most 0.0029.
Values may be sent and summed in bfloat16 or wider, within the bound.
A program may use at most 128 MiB of HBM per device.

v0:
```python
import jax
import jax.numpy as jnp
from jax import lax
from jax.sharding import PartitionSpec as P


def on_device(query_grads, train_grads, left_inverse, right_inverse):
    layers, rows, feat = query_grads.shape
    proj = left_inverse.shape[1]
    square = query_grads.astype(jnp.float32).reshape(layers, rows, proj, proj)
    rotated = jnp.einsum(
        "lab,lqbc,lcd->lqad", left_inverse, square, right_inverse, precision=lax.Precision.HIGHEST
    )
    rotated = rotated.reshape(layers, rows, feat).astype(jnp.bfloat16)
    partial_value = jnp.einsum(
        "lqf,ltf->qt",
        lax.all_gather(rotated, "row", axis=1, tiled=True),
        train_grads,
        preferred_element_type=jnp.float32,
    )
    summed = lax.psum(partial_value, "layer")
    block = summed.shape[0] // lax.axis_size("layer")
    return lax.dynamic_slice_in_dim(summed, lax.axis_index("layer") * block, block, 0)


def solution(mesh):
    placed = (
        P("layer", "row", None),
        P("layer", "row", None),
        P("layer", None, None),
        P("layer", None, None),
    )
    return jax.shard_map(
        on_device, mesh=mesh, in_specs=placed, out_specs=P("layer", "row"), check_vma=False
    )
```

profile of v0, /device:TPU:24, one launch (start us, length us, event | category | flops | bytes accessed | tf_op | source)
XLA Modules:
  0.0 275.1 jit_solution(14499633773549307910)
XLA Ops:
  6.5 0.0 copy-start
  6.5 0.0 copy-start.1
  6.5 0.0 all-gather.2.cloned.1.call-start
  6.5 2.1 reshape.5
  8.6 0.0 copy-done
  8.6 1.0 fusion.1
  9.6 0.0 copy-done.1
  9.6 1.9 convolution_convert_fusion
  11.5 1.6 convert_element_type.8
  13.2 0.0 all-gather.2.cloned.1.call-update
  13.2 0.0 all-reduce.2.cloned.1.call-start
  13.2 102.5 %all-gather.2.cloned.1.call-done = bf16[2,1024,4096]{2,1,0:T(8,128)(2,1)} async-done(((bf16[2,32,4096]{2,1,0:T(8,128)(2,1)}), bf16[2,1024,4096]{2,1,0:T(8,128)(2,1)}) %all-gather.2.cloned.1.call-update) | async-done | bytes 16777232 | tf_op jit(solution)/shard_map/all_gather | solution.py:17
  115.7 15.8 %convolution_bitcast_fusion = f32[1024,512]{1,0:T(8,128)} fusion(bf16[2,1024,4096]{2,1,0:T(8,128)(2,1)} %all-gather.2.cloned.1.call-done, bf16[2,512,4096]{2,1,0:T(8,128)(2,1)} %param.5), kind=kOutput, calls=%fused_computation | convolution fusion | flops 8589934592 | bytes 27262976 | tf_op jit(solution)/shard_map/lqf,ltf->qt/dot_general | solution.py:15
  131.6 0.0 all-reduce.2.cloned.1.call-update
  131.6 135.0 %all-reduce.2.cloned.1.call-done = f32[1024,512]{1,0:T(8,128)} async-done(((f32[1024,512]{1,0:T(8,128)}), f32[1024,512]{1,0:T(8,128)}) %all-reduce.2.cloned.1.call-update) | async-done | bytes 2097168 | tf_op jit(solution)/shard_map/psum | solution.py:21
  266.6 1.7 constant_dynamic-slice_fusion
Async XLA Ops:
  6.5 2.1 copy-start
  6.5 3.1 %copy-start.1 = (f32[2,64,64]{2,1,0:T(8,128)S(1)}, f32[2,64,64]{2,1,0:T(8,128)}, u32[]{:S(2)}) copy-start(f32[2,64,64]{2,1,0:T(8,128)} %param.7) | copy-start | bytes 98308
  6.5 109.2 %all-gather.2.cloned.1.call-start = ((), (), s32[]{:S(2)}) async-start(), calls=%async_computation | async-start | bytes 17301504 | tf_op jit(solution)/shard_map/all_gather | solution.py:17
  13.2 253.4 %all-reduce.2.cloned.1.call-start = ((), (), s32[]{:S(2)}) async-start(), calls=%async_computation.1 | async-start | bytes 4194304 | tf_op jit(solution)/shard_map/psum | solution.py:21
Sparse Core Ops, SparseCore 0:
  13.3 102.3 all-gather.1
  131.7 134.8 all-reduce.1
where the time goes:
time: 275 us
  waiting for transfers between devices  238 us (87%)
  matrix products  18.7 us (7%)
  between operations  13.4 us (5%)
  local copies, waits for them, and re-layouts  5.38 us (2%)
    psum x1, waiting for transfers between devices, on_device(): summed = lax.psum(partial_value, 'layer')  135 us
    all_gather x1, waiting for transfers between devices, on_device(): lax.all_gather(rotated, 'row', axis=1, tiled=True)  102 us
    dot_general x1, matrix products, on_device(): jnp.einsum('lqf,ltf->qt', lax.all_gather(rotated, 'row', axis=1, tiled=Tr...  15.8 us
  transfers between devices with their start and end apart: 2, of which 2 were waited for; matrix products, arithmetic and copies ran while one was open for 0% of the time, Pallas kernels for 0%

commit v1 on v0

--- a/solution.py
+++ b/solution.py
@@ -14,7 +14,9 @@
     rotated = rotated.reshape(layers, rows, feat).astype(jnp.bfloat16)
     partial_value = jnp.einsum(
         "lqf,ltf->qt",
-        lax.all_gather(rotated, "row", axis=1, tiled=True),
+        jnp.concatenate(
+            lax.all_to_all(jnp.stack([rotated] * lax.axis_size("row")), "row", 0, 0), axis=1
+        ),
         train_grads,
         preferred_element_type=jnp.float32,
     )

time: 275 us -> 552 us (2.01)
  blocking collectives: 0 us -> 374 us
  waiting for transfers between devices: 238 us -> 133 us
  local copies, waits for them, and re-layouts: 5.38 us -> 13.6 us
    all_to_all x0 -> x1, blocking collectives: none -> 374 us  [on_device(): lax.all_to_all(jnp.stack([rotated] * lax.axis_size('row')), 'row', 0, 0)]
    all_gather x1 -> x0, waiting for transfers between devices: 102 us -> none  [on_device(): lax.all_gather(rotated, 'row', axis=1, tiled=True)]
    reshape x0 -> x1, local copies, waits for them, and re-layouts: none -> 7.07 us  [on_device(): jnp.concatenate(lax.all_to_all(jnp.stack([rotated] * lax.axis_size('row')...]
  transfers between devices with their start and end apart: 2 -> 1, of which waited for: 2 -> 1; matrix products, arithmetic and copies ran while one was open for 0% -> 0% of each run, Pallas kernels for 0% -> 0%
where the time goes in v1:
time: 552 us
  blocking collectives  374 us (68%)
  waiting for transfers between devices  133 us (24%)
  matrix products  18 us (3%)
  local copies, waits for them, and re-layouts  13.6 us (2%)
  between operations  13.5 us (2%)
    all_to_all x1, blocking collectives, on_device(): lax.all_to_all(jnp.stack([rotated] * lax.axis_size('row')), 'row', 0, 0)  374 us
    psum x1, waiting for transfers between devices, on_device(): summed = lax.psum(partial_value, 'layer')  133 us
    dot_general x1, matrix products, on_device(): jnp.einsum('lqf,ltf->qt', jnp.concatenate(lax.all_to_all(jnp.stack([rotat...  14.3 us
  transfers between devices with their start and end apart: 1, of which 1 were waited for; matrix products, arithmetic and copies ran while one was open for 0% of the time, Pallas kernels for 0%

profile of v1, /device:TPU:24, one launch (start us, length us, event | category | flops | bytes accessed | tf_op | source)
XLA Modules:
  0.0 551.6 jit_solution(18000130470132529813)
XLA Ops:
  6.5 0.0 copy-start
  6.5 0.0 all-reduce.2.cloned.1.call-start
  6.5 2.1 reshape.14
  8.6 0.0 copy-done
  8.6 1.0 fusion.1
  9.6 2.7 convolution_convert_fusion
  12.4 0.8 convert_element_type.10
  13.2 2.0 stack.2
  15.2 0.0 slice-start
  15.2 373.7 %all_to_all.5 = bf16[32,2,32,4096]{3,2,1,0:T(8,128)(2,1)S(1)} all-to-all(bf16[32,2,32,4096]{3,2,1,0:T(8,128)(2,1)S(1)} %stack.2), channel_id=1, replica_groups=mesh['layer'=8,'row'=32] {'row'}, dimensions={0} | all-to-all | bytes 33554432 | tf_op jit(solution)/shard_map/all_to_all | solution.py:18
  388.9 0.0 slice-start.1
  388.9 7.1 %copy.5 = bf16[2,32,32,4096]{3,2,1,0:T(8,128)(2,1)} copy(bf16[2,32,32,4096]{3,2,0,1:T(8,128)(2,1)S(1)} %bitcast.20) | data formatting | bytes 33554432 | tf_op jit(solution)/shard_map/reshape | solution.py:17
  396.0 0.0 slice-done
  396.0 0.0 slice-done.1
  396.0 0.0 copy-start.1
  396.0 14.3 %convolution_bitcast_fusion = f32[1024,512]{1,0:T(8,128)} fusion(bf16[2,1024,4096]{2,1,0:T(8,128)(2,1)} %bitcast.21, bf16[2,512,4096]{2,1,0:T(8,128)(2,1)S(1)} %bitcast.23), kind=kOutput, calls=%fused_computation | convolution fusion | flops 8589934592 | bytes 27262976 | tf_op jit(solution)/shard_map/lqf,ltf->qt/dot_general | solution.py:15
  410.3 0.0 all-reduce.2.cloned.1.call-update
  410.4 132.7 %all-reduce.2.cloned.1.call-done = f32[1024,512]{1,0:T(8,128)} async-done(((f32[1024,512]{1,0:T(8,128)}), f32[1024,512]{1,0:T(8,128)}) %all-reduce.2.cloned.1.call-update) | async-done | bytes 2097168 | tf_op jit(solution)/shard_map/psum | solution.py:23
  543.1 1.7 constant_dynamic-slice_fusion
  544.7 0.0 copy-done.1
  (1 shorter events, 0.0 us)
Async XLA Ops:
  6.5 2.1 copy-start
  6.5 536.5 %all-reduce.2.cloned.1.call-start = ((), (), s32[]{:S(2)}) async-start(), calls=%async_computation.1 | async-start | bytes 4194304 | tf_op jit(solution)/shard_map/psum | solution.py:23
  15.2 380.8 %slice-start = ((s8[8388608]{0:T(1024)(128)(4,1)}), s8[4194304]{0:T(1024)(128)(4,1)S(1)}, s32[]{:S(2)}) async-start(s8[8388608]{0:T(1024)(128)(4,1)} %bitcast.22), calls=%async_computation.2 | async-start | bytes 8388608
  388.9 7.1 %slice-start.1 = ((s8[8388608]{0:T(1024)(128)(4,1)}), s8[4194304]{0:T(1024)(128)(4,1)S(1)}, s32[]{:S(2)}) async-start(s8[8388608]{0:T(1024)(128)(4,1)} %bitcast.22), calls=%async_computation.3 | async-start | bytes 8388608
  396.0 148.7 %copy-start.1 = (f32[2,64,64]{2,1,0:T(8,128)S(1)}, f32[2,64,64]{2,1,0:T(8,128)}, u32[]{:S(2)}) copy-start(f32[2,64,64]{2,1,0:T(8,128)} %param.6) | copy-start | bytes 98308
Sparse Core Ops, SparseCore 0:
  410.5 132.5 all-reduce.1

commit v2 on v0

--- a/solution.py
+++ b/solution.py
@@ -18,7 +18,7 @@
         train_grads,
         preferred_element_type=jnp.float32,
     )
-    summed = lax.psum(partial_value, "layer")
+    summed = jnp.sum(lax.all_gather(partial_value, "layer"), axis=0)
     block = summed.shape[0] // lax.axis_size("layer")
     return lax.dynamic_slice_in_dim(summed, lax.axis_index("layer") * block, block, 0)
 

time: 275 us -> 456 us (1.66)
  waiting for transfers between devices: 238 us -> 408 us
  other arithmetic: 0 us -> 8.08 us
    all_gather x0 -> x1, waiting for transfers between devices: none -> 306 us  [on_device(): summed = jnp.sum(lax.all_gather(partial_value, 'layer'), axis=0)]
    psum x1 -> x0, waiting for transfers between devices: 135 us -> none  [on_device(): summed = lax.psum(partial_value, 'layer')]
    reduce_sum x0 -> x1, other arithmetic: none -> 8.08 us  [on_device(): summed = jnp.sum(lax.all_gather(partial_value, 'layer'), axis=0)]
where the time goes in v2:
time: 456 us; the launch traced here: 453 us
  waiting for transfers between devices  408 us (89%)
  matrix products  18.7 us (4%)
  between operations  13.4 us (3%)
  other arithmetic  8.08 us (2%)
    all_gather x1, waiting for transfers between devices, on_device(): summed = jnp.sum(lax.all_gather(partial_value, 'layer'), axis=0)  306 us
    all_gather x1, waiting for transfers between devices, on_device(): lax.all_gather(rotated, 'row', axis=1, tiled=True)  102 us
    dot_general x1, matrix products, on_device(): jnp.einsum('lqf,ltf->qt', lax.all_gather(rotated, 'row', axis=1, tiled=Tr...  15.8 us
  transfers between devices with their start and end apart: 2, of which 2 were waited for; matrix products, arithmetic and copies ran while one was open for 0% of the time, Pallas kernels for 0%

profile of v2, /device:TPU:24, one launch (start us, length us, event | category | flops | bytes accessed | tf_op | source)
XLA Modules:
  0.0 453.2 jit_solution(7298761061838377699)
XLA Ops:
  6.5 0.0 copy-start
  6.5 0.0 copy-start.1
  6.5 0.0 all-gather.4.cloned.1.call-start
  6.5 2.1 reshape.5
  8.6 0.0 copy-done
  8.6 1.0 fusion.1
  9.6 0.0 copy-done.1
  9.6 1.9 convolution_convert_fusion
  11.5 1.6 convert_element_type.8
  13.2 0.0 all-gather.4.cloned.1.call-update
  13.2 0.0 all-gather.6.cloned.1.call-start
  13.2 102.5 %all-gather.4.cloned.1.call-done = bf16[2,1024,4096]{2,1,0:T(8,128)(2,1)} async-done(((bf16[2,32,4096]{2,1,0:T(8,128)(2,1)}), bf16[2,1024,4096]{2,1,0:T(8,128)(2,1)}) %all-gather.4.cloned.1.call-update) | async-done | bytes 16777232 | tf_op jit(solution)/shard_map/all_gather | solution.py:17
  115.7 15.8 %convolution_bitcast_fusion = f32[1024,512]{1,0:T(8,128)} fusion(bf16[2,1024,4096]{2,1,0:T(8,128)(2,1)} %all-gather.4.cloned.1.call-done, bf16[2,512,4096]{2,1,0:T(8,128)(2,1)} %param.5), kind=kOutput, calls=%fused_computation | convolution fusion | flops 8589934592 | bytes 27262976 | tf_op jit(solution)/shard_map/lqf,ltf->qt/dot_general | solution.py:15
  131.6 0.0 all-gather.6.cloned.1.call-update
  131.6 305.9 %all-gather.6.cloned.1.call-done = f32[8192,512]{1,0:T(8,128)} async-done(((f32[1024,512]{1,0:T(8,128)}), f32[8192,512]{1,0:T(8,128)}) %all-gather.6.cloned.1.call-update) | async-done | bytes 16777232 | tf_op jit(solution)/shard_map/all_gather | solution.py:21
  437.5 8.1 %reduce_sum.9 = f32[1024,512]{1,0:T(8,128)S(1)} reduce(f32[8,1024,512]{2,1,0:T(8,128)} %bitcast.19, f32[]{:T(128)} %constant.2.clone.1), dimensions={0}, to_apply=%region_0.0 | reduce | flops 3670016 | bytes 18874372 | tf_op jit(solution)/shard_map/reduce_sum | solution.py:21
  445.6 0.7 constant_dynamic-slice_fusion
Async XLA Ops:
  6.5 2.1 copy-start
  6.5 3.1 copy-start.1
  6.5 109.2 %all-gather.4.cloned.1.call-start = ((), (), s32[]{:S(2)}) async-start(), calls=%async_computation | async-start | bytes 17301504 | tf_op jit(solution)/shard_map/all_gather | solution.py:17
  13.2 424.3 %all-gather.6.cloned.1.call-start = ((), (), s32[]{:S(2)}) async-start(), calls=%async_computation.1 | async-start | bytes 18874368 | tf_op jit(solution)/shard_map/all_gather | solution.py:21
Sparse Core Ops, SparseCore 0:
  13.3 102.3 all-gather.3
  131.7 305.7 all-gather.5
